TPU v7x, 512 devices: a whole 4x8x8 slice. The times are simulated.
512 devices in a mesh: tok: 64 (over y, z_lo, x), feat: 8 (over z_hi, core).
Axes of the slice: x: 4, y: 8, z: 8 (z_hi: 4, z_lo: 2; z = z_hi * 2 + z_lo), core: 2. Of those that a mesh axis runs over, the one named last changes fastest.
Arguments:
- hidden_states: bfloat16 [110592, 8192], P('tok', 'feat'), may hold values from -60 to 60
- current_block: float32 [8192, 64], P('feat'), may hold values from -0.0625 to 0.0625
- directions: float32 [8192, 64], P('feat'), may hold values from -0.0625 to 0.0625
Outputs:
- block_image: float32 [8192, 192], P('feat')
- gram_image: float32 [192, 192], replicated
- gram_search: float32 [192, 192], replicated
All inputs are finite; a program needn't handle non-finite values.
Results may differ from a plain program's by a relative error of at most 0.005.
Values may be sent and summed in bfloat16 or wider, within the bound.
No kernel may reach another device: no remote copies, remote signals or barrier semaphores. Data moves between devices by JAX's collectives and lax.ppermute only.
A program may use at most 64 MiB of HBM per device.

v0:
```python
import math
import jax
import jax.numpy as jnp
from jax import lax
from jax.sharding import PartitionSpec as P

LAG = 256
SMALL = 2.0 ** (-20)
HIGHEST = lax.Precision.HIGHEST


def exchange(value, axis):
    return lax.all_to_all(value, axis, 0, 0, tiled=True)


def scattered_sum(value, axis):
    return jnp.sum(exchange(value, axis).astype(jnp.float32), axis=0)


def gathered(value, axis):
    return exchange(jnp.broadcast_to(value, (lax.axis_size(axis),) + value.shape), axis)


def rows_dot(a, b, **kwargs):
    return lax.dot_general(
        a, b, (((1,), (1,)), ((), ())), preferred_element_type=jnp.float32, **kwargs
    )


def local(hidden_states, current_block, directions):
    tokens, features = hidden_states.shape
    cols = current_block.shape[1]
    feat, tok = (lax.axis_size("feat"), lax.axis_size("tok"))
    factor = 0.5 / math.sqrt(tokens * tok - LAG)
    half = jnp.bfloat16
    up = [(i, i + 1) for i in range(tok - 1)]
    down = [(i + 1, i) for i in range(tok - 1)]
    behind = lax.ppermute(hidden_states[tokens - LAG :], "tok", up)
    ahead = lax.ppermute(hidden_states[:LAG], "tok", down)
    x, p = (current_block.T, directions.T)

    def project(vectors):
        pieces = [rows_dot(vectors, part) for part in (behind, hidden_states, ahead)]
        return jnp.concatenate(pieces, axis=1)

    def lagged(projected):
        return projected[:, 2 * LAG :] + projected[:, :tokens]

    def backward(lagged_rows):
        return lax.dot_general(
            lagged_rows, hidden_states, (((1,), (0,)), ((), ())), preferred_element_type=jnp.float32
        )

    side = lax.psum(
        jnp.concatenate(
            [
                project(p.astype(half)),
                rows_dot(p, jnp.concatenate([x, p]), precision=HIGHEST),
                rows_dot(x, x, precision=HIGHEST),
            ],
            axis=1,
        ),
        "feat",
    )
    part = lagged(project(x.astype(half)))
    own = scattered_sum(part.reshape(feat, cols // feat, tokens), "feat").astype(half)
    lag_x = gathered(own, "feat").reshape(cols, tokens)
    own = scattered_sum(backward(lag_x).reshape(tok, cols // tok, features), "tok") * factor
    image_x = gathered(own, "tok").reshape(cols, features)
    both = rows_dot(image_x, jnp.concatenate([x, p]), precision=HIGHEST)
    both = jnp.sum(gathered(both, "feat"), axis=0)
    rayleigh_t, image_x_p = (both[:, :cols], both[:, cols:])
    residual = (image_x - jnp.dot(rayleigh_t, x, precision=HIGHEST)) * SMALL
    width = tokens + 2 * LAG
    part = jnp.concatenate(
        [
            project(residual.astype(half)),
            rows_dot(residual, jnp.concatenate([x, residual, p]), precision=HIGHEST),
        ],
        axis=1,
    )
    own = scattered_sum(part.reshape(feat, cols // feat, part.shape[1]), "feat")
    high = own.astype(half)
    low = (own[:, width:] - high[:, width:].astype(jnp.float32)).astype(half)
    everything = gathered(jnp.concatenate([high, low], axis=1), "feat").reshape(cols, -1)
    proj_r = everything[:, :width]
    inner = everything[:, width:].astype(jnp.float32)
    inner = inner[:, : 3 * cols] + inner[:, 3 * cols :]
    r_x, r_r, r_p = (inner[:, i * cols : (i + 1) * cols] for i in range(3))
    proj_p = side[:, :width]
    lag_r = lagged(proj_r.astype(jnp.float32)).astype(half)
    lag_p = lagged(proj_p).astype(half)
    mid_r = proj_r[:, LAG : LAG + tokens]
    mid_p = proj_p[:, LAG : LAG + tokens].astype(half)
    image = backward(jnp.concatenate([lag_r, lag_p]))
    cross = rows_dot(jnp.concatenate([mid_r, mid_p]), jnp.concatenate([lag_r, lag_p]))
    part = jnp.concatenate(
        [
            image[:cols].reshape(tok, -1),
            image[cols:].reshape(tok, -1),
            cross[:cols, :cols].reshape(tok, -1),
            cross[cols:, :cols].reshape(tok, -1),
            cross[cols:, cols:].reshape(tok, -1),
        ],
        axis=1,
    )
    own = scattered_sum(part[:, None, :], "tok") * factor
    total = gathered(own, "tok")[:, 0, :]
    sizes = [cols * features // tok] * 2 + [cols * cols // tok] * 3
    ends = [sum(sizes[: i + 1]) for i in range(5)]
    image_r, image_p = (
        total[:, e - s : e].reshape(cols, features) for e, s in zip(ends[:2], sizes[:2])
    )
    c_rr, c_pr, c_pp = (
        total[:, e - s : e].reshape(cols, cols) for e, s in zip(ends[2:], sizes[2:])
    )
    lengths = jnp.sum(r_r * jnp.eye(cols, dtype=jnp.float32), axis=1, keepdims=True)
    scale = lax.rsqrt(lengths * (1.0 / SMALL**2) + 1e-06) * (1.0 / SMALL)
    across = scale.T
    block_image = jnp.concatenate([image_x, image_r * scale, image_p])
    u_x, u_p = (r_x * scale, r_p * scale)
    u_u = r_r * scale * across
    u_image_x = (r_r * (1.0 / SMALL) + jnp.dot(r_x, rayleigh_t.T, precision=HIGHEST)) * scale
    p_image_u = c_pr * across
    gram_image = jnp.concatenate(
        [
            jnp.concatenate([rayleigh_t.T, u_image_x.T, image_x_p], axis=1),
            jnp.concatenate([u_image_x, c_rr * scale * across, p_image_u.T], axis=1),
            jnp.concatenate([image_x_p.T, p_image_u, c_pp], axis=1),
        ]
    )
    p_x, p_p, x_x = (side[:, width + i * cols : width + (i + 1) * cols] for i in range(3))
    gram_search = jnp.concatenate(
        [
            jnp.concatenate([x_x, u_x.T, p_x.T], axis=1),
            jnp.concatenate([u_x, u_u, u_p], axis=1),
            jnp.concatenate([p_x, u_p.T, p_p], axis=1),
        ]
    )
    return (block_image.T, gram_image, gram_search)


def solution(mesh):
    return jax.shard_map(
        local,
        mesh=mesh,
        in_specs=(P("tok", "feat"), P("feat", None), P("feat", None)),
        out_specs=(P("feat", None), P(), P()),
        check_vma=False,
    )
```

profile of v0, /device:TPU:8, one launch (start us, length us, event | category | flops | bytes accessed | tf_op | source)
XLA Modules:
  0.0 323.3 jit_solution(342067930068575905)
XLA Ops:
  8.5 3.4 %collective-permute-start.1 = (bf16[256,1024]{1,0:T(8,128)(2,1)S(1)}, bf16[256,1024]{1,0:T(8,128)(2,1)S(1)}, u32[]{:S(2)}, u32[]{:S(2)}) collective-permute-start(bf16[256,1024]{1,0:T(8,128)(2,1)S(1)} %get-tuple-element.16), channel_id=1, source_target_pairs={{0,8},{8,16},{16,24},{24,32},{32,40},{40,48},{48,56},{56,64},{64,7... | collective-permute-start | bytes 1572872 | tf_op jit(solution)/shard_map/ppermute | solution.py:38
  11.9 5.5 %collective-permute-start = (bf16[256,1024]{1,0:T(8,128)(2,1)S(1)}, bf16[256,1024]{1,0:T(8,128)(2,1)S(1)}, u32[]{:S(2)}, u32[]{:S(2)}) collective-permute-start(bf16[256,1024]{1,0:T(8,128)(2,1)S(1)} %get-tuple-element.15), channel_id=1, source_target_pairs={{8,0},{16,8},{24,16},{32,24},{40,32},{48,40},{56,48},{64,56},{72,6... | collective-permute-start | bytes 1572872 | tf_op jit(solution)/shard_map/ppermute | solution.py:39
  17.4 3.2 fusion.49
  20.6 6.5 %collective-permute-done.1 = bf16[256,1024]{1,0:T(8,128)(2,1)S(1)} collective-permute-done((bf16[256,1024]{1,0:T(8,128)(2,1)S(1)}, bf16[256,1024]{1,0:T(8,128)(2,1)S(1)}, u32[]{:S(2)}, u32[]{:S(2)}) %collective-permute-start.1) | collective-permute-done | bytes 524320 | tf_op jit(solution)/shard_map/ppermute | solution.py:38
  29.2 26.6 %all_to_all.45 = f32[8,8,1728]{2,1,0:T(8,128)} all-to-all(f32[8,8,1728]{2,1,0:T(8,128)S(1)} %fusion.12), channel_id=1, replica_groups=mesh['tok'=64,'feat'=8] {'feat'}, dimensions={0} | all-to-all | bytes 884736 | tf_op jit(solution)/shard_map/all_to_all | solution.py:13
  55.8 1.7 reduce_sum.54
  58.2 14.3 %all_to_all.46 = bf16[8,8,1728]{2,1,0:T(8,128)(2,1)S(1)} all-to-all(bf16[8,8,1728]{2,1,0:T(8,128)(2,1)S(1)} %broadcast_in_dim.19), channel_id=1, replica_groups=mesh['tok'=64,'feat'=8] {'feat'}, dimensions={0} | all-to-all | bytes 442368 | tf_op jit(solution)/shard_map/all_to_all | solution.py:13
  73.5 22.8 %all_to_all.47 = f32[64,1,1024]{2,1,0:T(1,128)} all-to-all(f32[64,1,1024]{2,1,0:T(1,128)S(1)} %copy.65), channel_id=1, replica_groups=mesh['tok'=64,'feat'=8] {'tok'}, dimensions={0} | all-to-all | bytes 524288 | tf_op jit(solution)/shard_map/all_to_all | solution.py:13
  97.7 16.2 %all_to_all.48 = f32[64,1,1024]{2,1,0:T(1,128)S(1)} all-to-all(f32[64,1,1024]{2,1,0:T(1,128)S(1)} %broadcast_in_dim.20), channel_id=1, replica_groups=mesh['tok'=64,'feat'=8] {'tok'}, dimensions={0} | all-to-all | bytes 524288 | tf_op jit(solution)/shard_map/all_to_all | solution.py:13
  114.5 1.7 fusion.17
  116.3 16.4 %all_to_all.49 = f32[8,64,128]{2,1,0:T(8,128)} all-to-all(f32[8,64,128]{2,1,0:T(8,128)S(1)} %broadcast_in_dim.21), channel_id=1, replica_groups=mesh['tok'=64,'feat'=8] {'feat'}, dimensions={0} | all-to-all | bytes 524288 | tf_op jit(solution)/shard_map/all_to_all | solution.py:13
  132.6 1.6 reduce_sum.56
  135.7 2.0 fusion.32
  137.6 1.5 fusion.5
  141.0 2.0 concatenate.65
  143.0 4.2 %all-to-all-start.5 = ((f32[8,8,2432]{2,1,0:T(8,128)}), f32[8,8,2432]{2,1,0:T(8,128)}, u32[]{:S(2)}, u32[]{:S(2)}) async-start(f32[8,8,2432]{2,1,0:T(8,128)} %bitcast.123), calls=%async_computation.5 | async-start | bytes 1245184 | tf_op jit(solution)/shard_map/all_to_all | solution.py:13
  147.2 2.1 convolution_dynamic-update-slice_fusion.2
  149.3 3.0 convolution_dynamic-update-slice_fusion
  155.4 11.6 %all-to-all-done.5 = f32[8,8,2432]{2,1,0:T(8,128)} async-done(((f32[8,8,2432]{2,1,0:T(8,128)}), f32[8,8,2432]{2,1,0:T(8,128)}, u32[]{:S(2)}, u32[]{:S(2)}) %all-to-all-start.5) | async-done | bytes 622624 | tf_op jit(solution)/shard_map/all_to_all | solution.py:13
  167.0 1.7 reduce_sum.57
  171.2 4.3 %all-to-all-start.6 = ((bf16[8,8,2624]{2,1,0:T(8,128)(2,1)}), bf16[8,8,2624]{2,1,0:T(8,128)(2,1)}, u32[]{:S(2)}, u32[]{:S(2)}) async-start(bf16[8,8,2624]{2,1,0:T(8,128)(2,1)} %broadcast_in_dim.22), calls=%async_computation.6 | async-start | bytes 688128 | tf_op jit(solution)/shard_map/all_to_all | solution.py:13
  175.4 65.7 %all-reduce.2.cloned.1.call-done = f32[64,2432]{0,1:T(8,128)} async-done(((f32[64,2432]{0,1:T(8,128)}), f32[64,2432]{0,1:T(8,128)}) %all-reduce.2.cloned.1.call-update) | async-done | bytes 622608 | tf_op jit(solution)/shard_map/psum | solution.py:54
  241.1 2.0 slice.200
  243.1 2.3 fusion.3
  245.4 1.7 slice.145
  247.1 1.7 slice.152
  248.7 2.0 copy.96
  252.7 1.9 copy.97
  254.6 2.2 fusion.19
  258.4 28.5 %all_to_all.50 = f32[64,1,2240]{2,1,0:T(1,128)S(1)} all-to-all(f32[64,1,2240]{2,1,0:T(1,128)S(1)} %copy.74), channel_id=1, replica_groups=mesh['tok'=64,'feat'=8] {'tok'}, dimensions={0} | all-to-all | bytes 1146880 | tf_op jit(solution)/shard_map/all_to_all | solution.py:13
  288.4 6.2 %all-to-all-start.8 = ((f32[64,1,2240]{2,1,0:T(1,128)}), f32[64,1,2240]{2,1,0:T(1,128)S(1)}, u32[]{:S(2)}, u32[]{:S(2)}) async-start(f32[64,1,2240]{2,1,0:T(1,128)} %broadcast_in_dim.24), calls=%async_computation.8 | async-start | bytes 1179648 | tf_op jit(solution)/shard_map/all_to_all | solution.py:13
  296.3 15.7 %all-to-all-done.8 = f32[64,1,2240]{2,1,0:T(1,128)S(1)} async-done(((f32[64,1,2240]{2,1,0:T(1,128)}), f32[64,1,2240]{2,1,0:T(1,128)S(1)}, u32[]{:S(2)}, u32[]{:S(2)}) %all-to-all-start.8) | async-done | bytes 573472 | tf_op jit(solution)/shard_map/all_to_all | solution.py:13
  (100 shorter events, 27.0 us)
Async XLA Ops:
  7.2 10.2 %copy-start.1 = (f32[1024,64]{0,1:T(8,128)S(1)}, f32[1024,64]{0,1:T(8,128)}, u32[]{:S(2)}) copy-start(f32[1024,64]{0,1:T(8,128)} %param.4) | copy-start | bytes 786436
  8.5 18.6 %collective-permute-start.1 = (bf16[256,1024]{1,0:T(8,128)(2,1)S(1)}, bf16[256,1024]{1,0:T(8,128)(2,1)S(1)}, u32[]{:S(2)}, u32[]{:S(2)}) collective-permute-start(bf16[256,1024]{1,0:T(8,128)(2,1)S(1)} %get-tuple-element.16), channel_id=1, source_target_pairs={{0,8},{8,16},{16,24},{24,32},{32,40},{40,48},{48,56},{56,64},{64,7... | collective-permute-start | bytes 1572872 | tf_op jit(solution)/shard_map/ppermute | solution.py:38
  11.9 16.3 %collective-permute-start = (bf16[256,1024]{1,0:T(8,128)(2,1)S(1)}, bf16[256,1024]{1,0:T(8,128)(2,1)S(1)}, u32[]{:S(2)}, u32[]{:S(2)}) collective-permute-start(bf16[256,1024]{1,0:T(8,128)(2,1)S(1)} %get-tuple-element.15), channel_id=1, source_target_pairs={{8,0},{16,8},{24,16},{32,24},{40,32},{48,40},{56,48},{64,56},{72,6... | collective-permute-start | bytes 1572872 | tf_op jit(solution)/shard_map/ppermute | solution.py:39
  27.1 2.1 copy-start.6
  28.2 0.8 copy-start.8
  28.2 44.3 %copy-start = (bf16[1728,1024]{1,0:T(8,128)(2,1)S(1)}, bf16[1728,1024]{1,0:T(8,128)(2,1)}, u32[]{:S(2)}) copy-start(bf16[1728,1024]{1,0:T(8,128)(2,1)} %param.3) | copy-start | bytes 10616836
  113.8 0.7 copy-start.11
  135.6 2.0 copy-start.2
  135.7 2.0 copy-start.4
  137.6 1.5 copy-start.7
  137.6 2.4 copy-start.9
  143.0 24.0 %all-to-all-start.5 = ((f32[8,8,2432]{2,1,0:T(8,128)}), f32[8,8,2432]{2,1,0:T(8,128)}, u32[]{:S(2)}, u32[]{:S(2)}) async-start(f32[8,8,2432]{2,1,0:T(8,128)} %bitcast.123), calls=%async_computation.5 | async-start | bytes 1245184 | tf_op jit(solution)/shard_map/all_to_all | solution.py:13
  147.2 93.9 %all-reduce.2.cloned.1.call-start = ((), (), s32[]{:S(2)}) async-start(), calls=%async_computation.9 | async-start | bytes 2490368 | tf_op jit(solution)/shard_map/psum | solution.py:54
  149.3 3.0 copy-start.5
  149.3 3.0 copy-start.10
  149.3 4.0 %copy-start.3 = (f32[1024,64]{0,1:T(8,128)S(1)}, f32[1024,64]{0,1:T(8,128)}, u32[]{:S(2)}) copy-start(f32[1024,64]{0,1:T(8,128)} %param.4) | copy-start | bytes 786436
  171.2 74.2 %all-to-all-start.6 = ((bf16[8,8,2624]{2,1,0:T(8,128)(2,1)}), bf16[8,8,2624]{2,1,0:T(8,128)(2,1)}, u32[]{:S(2)}, u32[]{:S(2)}) async-start(bf16[8,8,2624]{2,1,0:T(8,128)(2,1)} %broadcast_in_dim.22), calls=%async_computation.6 | async-start | bytes 688128 | tf_op jit(solution)/shard_map/all_to_all | solution.py:13
  254.6 2.3 copy-start.13
  254.6 2.3 copy-start.14
  254.6 2.3 copy-start.15
  254.6 2.3 copy-start.16
  286.9 7.7 %copy-start.12 = (f32[64,1,1024]{2,1,0:T(1,128)S(1)}, f32[64,1,1024]{2,1,0:T(1,128)}, u32[]{:S(2)}) copy-start(f32[64,1,1024]{2,1,0:T(1,128)} %copy-done.11) | copy-start | bytes 786436
  287.3 7.4 %copy-start.17 = (f32[64,128]{1,0:T(8,128)S(1)}, f32[64,128]{1,0:T(8,128)}, u32[]{:S(2)}) copy-start(f32[64,128]{1,0:T(8,128)} %reduce_sum.56) | copy-start | bytes 98308
  288.4 23.7 %all-to-all-start.8 = ((f32[64,1,2240]{2,1,0:T(1,128)}), f32[64,1,2240]{2,1,0:T(1,128)S(1)}, u32[]{:S(2)}, u32[]{:S(2)}) async-start(f32[64,1,2240]{2,1,0:T(1,128)} %broadcast_in_dim.24), calls=%async_computation.8 | async-start | bytes 1179648 | tf_op jit(solution)/shard_map/all_to_all | solution.py:13
Sparse Core Ops, SparseCore 0:
  155.5 85.4 all-reduce.1
where the time goes:
time: 325 us; the launch traced here: 323 us
  blocking collectives  125 us (38%)
  waiting for transfers between devices  100 us (31%)
  matrix products  24.1 us (7%)
  starting transfers between devices  23.6 us (7%)
  local copies, waits for them, and re-layouts  20.5 us (6%)
  other arithmetic  15.5 us (5%)
  between operations  14.4 us (4%)
    all_to_all x6, blocking collectives, exchange(): return lax.all_to_all(value, axis, 0, 0, tiled=True)  125 us
    psum x1, waiting for transfers between devices, local(): lax.psum(jnp.concatenate([project(p.astype(half)), rows_dot(p, jnp.concat...  65.7 us
    all_to_all x3, waiting for transfers between devices, exchange(): return lax.all_to_all(value, axis, 0, 0, tiled=True)  27.3 us
    dot_general x14, matrix products, rows_dot(): lax.dot_general(a, b, (((1,), (1,)), ((), ())), preferred_element_type=jn...  19.6 us
    all_to_all x3, starting transfers between devices, exchange(): return lax.all_to_all(value, axis, 0, 0, tiled=True)  14.7 us
    unnamed x47, local copies, waits for them, and re-layouts  6.63 us
  transfers between devices with their start and end apart: 6, of which 5 were waited for; matrix products, arithmetic and copies ran while one was open for 7% of the time, Pallas kernels for 0%

commit v1 on v0

--- a/solution.py
+++ b/solution.py
@@ -51,16 +51,19 @@
             lagged_rows, hidden_states, (((1,), (0,)), ((), ())), preferred_element_type=jnp.float32
         )
 
-    side = lax.psum(
-        jnp.concatenate(
-            [
-                project(p.astype(half)),
-                rows_dot(p, jnp.concatenate([x, p]), precision=HIGHEST),
-                rows_dot(x, x, precision=HIGHEST),
-            ],
-            axis=1,
+    side = jnp.sum(
+        lax.all_gather(
+            jnp.concatenate(
+                [
+                    project(p.astype(half)),
+                    rows_dot(p, jnp.concatenate([x, p]), precision=HIGHEST),
+                    rows_dot(x, x, precision=HIGHEST),
+                ],
+                axis=1,
+            ),
+            "feat",
         ),
-        "feat",
+        axis=0,
     )
     part = lagged(project(x.astype(half)))
     own = scattered_sum(part.reshape(feat, cols // feat, tokens), "feat").astype(half)

time: 325 us -> 289 us (0.89)
  waiting for transfers between devices: 100 us -> 34.9 us
  blocking collectives: 125 us -> 156 us
  local copies, waits for them, and re-layouts: 20.5 us -> 16.1 us
    psum x1 -> x0, waiting for transfers between devices: 65.7 us -> none  [local(): lax.psum(jnp.concatenate([project(p.astype(half)), rows_dot(p, jnp.concat...]
    all_to_all x6 -> x7, blocking collectives: 125 us -> 156 us  [exchange(): return lax.all_to_all(value, axis, 0, 0, tiled=True)]
    all_to_all x3 -> x2, waiting for transfers between devices: 27.3 us -> 33.7 us  [exchange(): return lax.all_to_all(value, axis, 0, 0, tiled=True)]
    ppermute x1, waiting for transfers between devices: 6.49 us -> 1.24 us  [local(): behind = lax.ppermute(hidden_states[tokens - LAG:], 'tok', up)]
    dot_general x14, matrix products: 19.6 us -> 23.4 us  [rows_dot(): lax.dot_general(a, b, (((1,), (1,)), ((), ())), preferred_element_type=jn...]
    reduce_sum x0 -> x1, other arithmetic: none -> 3.54 us  [local(): jnp.sum(lax.all_gather(jnp.concatenate([project(p.astype(half)), rows_dot...]
    unnamed x47 -> x29, local copies, waits for them, and re-layouts: 6.63 us -> 3.56 us
    all_to_all x3 -> x2, starting transfers between devices: 14.7 us -> 12 us  [exchange(): return lax.all_to_all(value, axis, 0, 0, tiled=True)]
  transfers between devices with their start and end apart: 6 -> 5, of which waited for: 5 -> 3; matrix products, arithmetic and copies ran while one was open for 7% -> 14% of each run, Pallas kernels for 0% -> 0%
where the time goes in v1:
time: 289 us; the launch traced here: 288 us
  blocking collectives  156 us (54%)
  waiting for transfers between devices  34.9 us (12%)
  matrix products  27.3 us (9%)
  starting transfers between devices  21 us (7%)
  other arithmetic  18.3 us (6%)
  local copies, waits for them, and re-layouts  16.1 us (6%)
  between operations  14.4 us (5%)
    all_to_all x7, blocking collectives, exchange(): return lax.all_to_all(value, axis, 0, 0, tiled=True)  156 us
    all_to_all x2, waiting for transfers between devices, exchange(): return lax.all_to_all(value, axis, 0, 0, tiled=True)  33.7 us
    dot_general x14, matrix products, rows_dot(): lax.dot_general(a, b, (((1,), (1,)), ((), ())), preferred_element_type=jn...  23.4 us
    all_to_all x2, starting transfers between devices, exchange(): return lax.all_to_all(value, axis, 0, 0, tiled=True)  12 us
  transfers between devices with their start and end apart: 5, of which 3 were waited for; matrix products, arithmetic and copies ran while one was open for 14% of the time, Pallas kernels for 0%

profile of v1, /device:TPU:8, one launch (start us, length us, event | category | flops | bytes accessed | tf_op | source)
XLA Modules:
  0.0 288.1 jit_solution(17448575841425468818)
XLA Ops:
  7.2 1.4 fusion.47
  8.7 3.4 %collective-permute-start.1 = (bf16[256,1024]{1,0:T(8,128)(2,1)S(1)}, bf16[256,1024]{1,0:T(8,128)(2,1)S(1)}, u32[]{:S(2)}, u32[]{:S(2)}) collective-permute-start(bf16[256,1024]{1,0:T(8,128)(2,1)S(1)} %get-tuple-element.16), channel_id=1, source_target_pairs={{0,8},{8,16},{16,24},{24,32},{32,40},{40,48},{48,56},{56,64},{64,7... | collective-permute-start | bytes 1572872 | tf_op jit(solution)/shard_map/ppermute | solution.py:38
  12.1 5.6 %collective-permute-start = (bf16[256,1024]{1,0:T(8,128)(2,1)S(1)}, bf16[256,1024]{1,0:T(8,128)(2,1)S(1)}, u32[]{:S(2)}, u32[]{:S(2)}) collective-permute-start(bf16[256,1024]{1,0:T(8,128)(2,1)S(1)} %get-tuple-element.15), channel_id=1, source_target_pairs={{8,0},{16,8},{24,16},{32,24},{40,32},{48,40},{56,48},{64,56},{72,6... | collective-permute-start | bytes 1572872 | tf_op jit(solution)/shard_map/ppermute | solution.py:39
  17.7 4.1 %fusion.58 = f32[64,1728]{1,0:T(8,128)} fusion(bf16[1728,1024]{1,0:T(8,128)(2,1)} %param.3, f32[1024,64]{0,1:T(8,128)} %param.5), kind=kOutput, calls=%fused_computation.90 | convolution fusion | flops 226492416 | bytes 4243456 | tf_op jit(solution)/shard_map/dot_general | solution.py:25
  21.7 2.0 fusion.50
  30.7 2.0 concatenate.67
  32.6 1.4 fusion.54
  34.0 1.4 fusion.52
  36.7 28.0 %all_to_all.45 = f32[8,8,1728]{2,1,0:T(8,128)} all-to-all(f32[8,8,1728]{2,1,0:T(8,128)S(1)} %fusion.11), channel_id=1, replica_groups=mesh['tok'=64,'feat'=8] {'feat'}, dimensions={0} | all-to-all | bytes 884736 | tf_op jit(solution)/shard_map/all_to_all | solution.py:13
  64.7 1.7 reduce_sum.63
  67.2 32.5 %all_to_all.46 = bf16[8,8,1728]{2,1,0:T(8,128)(2,1)S(1)} all-to-all(bf16[8,8,1728]{2,1,0:T(8,128)(2,1)S(1)} %broadcast_in_dim.19), channel_id=1, replica_groups=mesh['tok'=64,'feat'=8] {'feat'}, dimensions={0} | all-to-all | bytes 442368 | tf_op jit(solution)/shard_map/all_to_all | solution.py:13
  100.7 20.0 %all_to_all.47 = f32[64,1,1024]{2,1,0:T(1,128)} all-to-all(f32[64,1,1024]{2,1,0:T(1,128)S(1)} %copy.47), channel_id=1, replica_groups=mesh['tok'=64,'feat'=8] {'tok'}, dimensions={0} | all-to-all | bytes 524288 | tf_op jit(solution)/shard_map/all_to_all | solution.py:13
  121.9 17.2 %all_to_all.48 = f32[64,1,1024]{2,1,0:T(1,128)S(1)} all-to-all(f32[64,1,1024]{2,1,0:T(1,128)S(1)} %broadcast_in_dim.20), channel_id=1, replica_groups=mesh['tok'=64,'feat'=8] {'tok'}, dimensions={0} | all-to-all | bytes 524288 | tf_op jit(solution)/shard_map/all_to_all | solution.py:13
  139.8 1.7 fusion.16
  141.5 17.6 %all_to_all.49 = f32[8,64,128]{2,1,0:T(8,128)} all-to-all(f32[8,64,128]{2,1,0:T(8,128)S(1)} %broadcast_in_dim.21), channel_id=1, replica_groups=mesh['tok'=64,'feat'=8] {'feat'}, dimensions={0} | all-to-all | bytes 524288 | tf_op jit(solution)/shard_map/all_to_all | solution.py:13
  159.1 1.6 reduce_sum.65
  160.6 1.4 fusion
  162.1 2.5 fusion.2
  164.6 2.0 fusion.39
  166.6 2.0 fusion.35
  168.5 2.0 fusion.37
  170.5 2.0 concatenate.65
  172.5 24.0 %all_to_all.50 = f32[8,8,2432]{2,1,0:T(8,128)} all-to-all(f32[8,8,2432]{2,1,0:T(8,128)} %bitcast.123), channel_id=1, replica_groups=mesh['tok'=64,'feat'=8] {'feat'}, dimensions={0} | all-to-all | bytes 1245184 | tf_op jit(solution)/shard_map/all_to_all | solution.py:13
  196.5 1.7 reduce_sum.66
  200.0 16.7 %all_to_all.51 = bf16[8,8,2624]{2,1,0:T(8,128)(2,1)S(1)} all-to-all(bf16[8,8,2624]{2,1,0:T(8,128)(2,1)S(1)} %broadcast_in_dim.22), channel_id=1, replica_groups=mesh['tok'=64,'feat'=8] {'feat'}, dimensions={0} | all-to-all | bytes 671744 | tf_op jit(solution)/shard_map/all_to_all | solution.py:13
  218.3 3.5 %reduce_sum.67 = f32[64,2432]{1,0:T(8,128)} reduce(f32[8,64,2432]{2,1,0:T(8,128)} %bitcast.120, f32[]{:T(128)} %constant.6.clone.1), dimensions={0}, to_apply=%region_4.0 | reduce | flops 1089536 | bytes 5603332 | tf_op jit(solution)/shard_map/reduce_sum | solution.py:54
  224.2 1.6 fusion.17
  226.3 1.4 copy.48
  227.7 5.7 %all-to-all-start.7 = ((f32[64,1,2240]{2,1,0:T(1,128)}), f32[64,1,2240]{2,1,0:T(1,128)S(1)}, u32[]{:S(2)}, u32[]{:S(2)}) async-start(f32[64,1,2240]{2,1,0:T(1,128)} %copy.48), calls=%async_computation.7 | async-start | bytes 1179648 | tf_op jit(solution)/shard_map/all_to_all | solution.py:13
  234.6 17.5 %all-to-all-done.7 = f32[64,1,2240]{2,1,0:T(1,128)S(1)} async-done(((f32[64,1,2240]{2,1,0:T(1,128)}), f32[64,1,2240]{2,1,0:T(1,128)S(1)}, u32[]{:S(2)}, u32[]{:S(2)}) %all-to-all-start.7) | async-done | bytes 573472 | tf_op jit(solution)/shard_map/all_to_all | solution.py:13
  253.6 6.3 %all-to-all-start.8 = ((f32[64,1,2240]{2,1,0:T(1,128)}), f32[64,1,2240]{2,1,0:T(1,128)S(1)}, u32[]{:S(2)}, u32[]{:S(2)}) async-start(f32[64,1,2240]{2,1,0:T(1,128)} %broadcast_in_dim.24), calls=%async_computation.8 | async-start | bytes 1179648 | tf_op jit(solution)/shard_map/all_to_all | solution.py:13
  261.7 16.2 %all-to-all-done.8 = f32[64,1,2240]{2,1,0:T(1,128)S(1)} async-done(((f32[64,1,2240]{2,1,0:T(1,128)}), f32[64,1,2240]{2,1,0:T(1,128)S(1)}, u32[]{:S(2)}, u32[]{:S(2)}) %all-to-all-start.8) | async-done | bytes 573472 | tf_op jit(solution)/shard_map/all_to_all | solution.py:13
  (83 shorter events, 25.7 us)
Async XLA Ops:
  7.2 14.6 %copy-start = (bf16[1728,1024]{1,0:T(8,128)(2,1)S(1)}, bf16[1728,1024]{1,0:T(8,128)(2,1)}, u32[]{:S(2)}) copy-start(bf16[1728,1024]{1,0:T(8,128)(2,1)} %param.3) | copy-start | bytes 10616836
  7.2 211.1 %all-gather.3.cloned.1.call-start = ((), (), s32[]{:S(2)}) async-start(), calls=%async_computation.9 | async-start | bytes 5603328 | tf_op jit(solution)/shard_map/all_gather | solution.py:55
  7.2 14.5 %copy-start.1 = (f32[1024,64]{0,1:T(8,128)S(1)}, f32[1024,64]{0,1:T(8,128)}, u32[]{:S(2)}) copy-start(f32[1024,64]{0,1:T(8,128)} %param.4) | copy-start | bytes 786436
  8.7 18.6 %collective-permute-start.1 = (bf16[256,1024]{1,0:T(8,128)(2,1)S(1)}, bf16[256,1024]{1,0:T(8,128)(2,1)S(1)}, u32[]{:S(2)}, u32[]{:S(2)}) collective-permute-start(bf16[256,1024]{1,0:T(8,128)(2,1)S(1)} %get-tuple-element.16), channel_id=1, source_target_pairs={{0,8},{8,16},{16,24},{24,32},{32,40},{40,48},{48,56},{56,64},{64,7... | collective-permute-start | bytes 1572872 | tf_op jit(solution)/shard_map/ppermute | solution.py:38
  12.1 11.7 %copy-start.2 = (f32[1024,64]{0,1:T(8,128)S(1)}, f32[1024,64]{0,1:T(8,128)}, u32[]{:S(2)}) copy-start(f32[1024,64]{0,1:T(8,128)} %param.5) | copy-start | bytes 786436
  12.1 16.9 %collective-permute-start = (bf16[256,1024]{1,0:T(8,128)(2,1)S(1)}, bf16[256,1024]{1,0:T(8,128)(2,1)S(1)}, u32[]{:S(2)}, u32[]{:S(2)}) collective-permute-start(bf16[256,1024]{1,0:T(8,128)(2,1)S(1)} %get-tuple-element.15), channel_id=1, source_target_pairs={{8,0},{16,8},{24,16},{32,24},{40,32},{48,40},{56,48},{64,56},{72,6... | collective-permute-start | bytes 1572872 | tf_op jit(solution)/shard_map/ppermute | solution.py:39
  27.2 0.8 copy-start.3
  28.9 0.8 copy-start.4
  139.1 0.7 copy-start.5
  216.7 0.8 copy-start.7
  221.8 3.9 %copy-start.8 = (bf16[64,1728]{1,0:T(8,128)(2,1)S(1)}, bf16[64,1728]{1,0:T(8,128)(2,1)}, u32[]{:S(2)}) copy-start(bf16[64,1728]{1,0:T(8,128)(2,1)} %fusion.9) | copy-start | bytes 663556
  221.8 3.9 %copy-start.10 = (bf16[64,1728]{1,0:T(8,128)(2,1)S(1)}, bf16[64,1728]{1,0:T(8,128)(2,1)}, u32[]{:S(2)}) copy-start(bf16[64,1728]{1,0:T(8,128)(2,1)} %slice.152) | copy-start | bytes 663556
  225.8 7.7 %copy-start.6 = (f32[64,1,1024]{2,1,0:T(1,128)S(1)}, f32[64,1,1024]{2,1,0:T(1,128)}, u32[]{:S(2)}) copy-start(f32[64,1,1024]{2,1,0:T(1,128)} %copy-done.5) | copy-start | bytes 786436
  225.8 7.7 %copy-start.9 = (f32[64,128]{1,0:T(8,128)S(1)}, f32[64,128]{1,0:T(8,128)}, u32[]{:S(2)}) copy-start(f32[64,128]{1,0:T(8,128)} %reduce_sum.65) | copy-start | bytes 98308
  227.7 24.4 %all-to-all-start.7 = ((f32[64,1,2240]{2,1,0:T(1,128)}), f32[64,1,2240]{2,1,0:T(1,128)S(1)}, u32[]{:S(2)}, u32[]{:S(2)}) async-start(f32[64,1,2240]{2,1,0:T(1,128)} %copy.48), calls=%async_computation.7 | async-start | bytes 1179648 | tf_op jit(solution)/shard_map/all_to_all | solution.py:13
  253.6 24.2 %all-to-all-start.8 = ((f32[64,1,2240]{2,1,0:T(1,128)}), f32[64,1,2240]{2,1,0:T(1,128)S(1)}, u32[]{:S(2)}, u32[]{:S(2)}) async-start(f32[64,1,2240]{2,1,0:T(1,128)} %broadcast_in_dim.24), calls=%async_computation.8 | async-start | bytes 1179648 | tf_op jit(solution)/shard_map/all_to_all | solution.py:13
Sparse Core Ops, SparseCore 0:
  32.8 75.7 all-gather.2
